TPU v7x, 512 devices: a whole 4x4x16 slice. The times are simulated.
512 devices in a mesh: wide: 64 (over z, x), narrow: 8 (over y, core).
Axes of the slice: x: 4, y: 4, z: 16, core: 2. Of those that a mesh axis runs over, the one named last changes fastest.
Arguments:
- hidden: bfloat16 [2048, 8192], P('wide', 'narrow'), may hold values from -6 to 6
- norm_gain: float32 [8192], P('narrow'), may hold values from 0.1 to 1.9
- head_weight: bfloat16 [8192, 32000], P('narrow', 'wide'), may hold values from -0.24 to 0.24
- diff_rows: bfloat16 [64, 8, 8, 32000], P('wide', 'narrow'), may hold values from -6 to 480
- slot_request: int32 [64, 8, 8], replicated, may hold values from 0 to 2047, as said below
- slot_code: int32 [64, 8, 8], replicated, may hold values from 1 to 8
- slot_count: int32 [64, 8], replicated, may hold values from 1 to 8, as said below
Outputs:
- log_probs: float32 [2048, 32000], P('narrow', 'wide')
Inputs may be any that keep to these rules, and one draw needn't show every extreme that they name: `slot_request`: within one pair, every request is named at most once. `slot_count`: slots at or beyond the count hold no row to use; in every draw some device uses all 8 slots.
All inputs are finite; a program needn't handle non-finite values.
Results may differ from a plain program's by a relative error of at most 0.0003.
Values may be sent and summed in bfloat16 or wider, within the bound.
A program may use at most 64 MiB of HBM per device.

v0:
```python
import jax
import jax.numpy as jnp
from jax import lax
from jax.sharding import PartitionSpec as P

D = 8192
epsilon = 1e-05


def combined_all(part, axis, combine):
    gathered = jax.tree.map(lambda a: lax.all_gather(a, axis), part)

    def take(source):
        return jax.tree.map(lambda a: lax.dynamic_index_in_dim(a, source, 0, False), gathered)

    return lax.fori_loop(
        1, lax.axis_size(axis), lambda source, state: combine(state, take(source)), take(0)
    )


def merge_pair(earlier, later):
    row_peak = jnp.maximum(earlier[0], later[0])
    summed = earlier[1] * jnp.exp(earlier[0] - row_peak) + later[1] * jnp.exp(later[0] - row_peak)
    return (row_peak, summed)


def body(hidden, norm_gain, head_weight, diff_rows, slot_request, slot_code, slot_count):
    values = hidden.astype(jnp.float32)
    squares = lax.psum(jnp.sum(values * values, axis=1), "narrow")
    scales = lax.rsqrt(squares / D + epsilon)
    normed = (values * scales[:, None] * norm_gain[None, :]).astype(jnp.bfloat16)
    partial_value = jnp.dot(
        lax.all_gather(normed, "wide", axis=0, tiled=True),
        head_weight,
        preferred_element_type=jnp.float32,
    )
    row_block = diff_rows[0, 0]
    arrived = lax.all_to_all(row_block, "wide", split_axis=1, concat_axis=0, tiled=True)
    slot_total = row_block.shape[0]
    active = jnp.arange(slot_total, dtype=jnp.int32)[None, None, :] < slot_count[:, :, None]
    weights = jnp.where(active, slot_code, 0).astype(jnp.float32) * 0.25
    base_block = lax.psum_scatter(partial_value, "narrow", scatter_dimension=0, tiled=True)
    owner_slices = lax.all_gather(arrived, "narrow", axis=0, tiled=True)
    targets = jnp.transpose(slot_request, (1, 0, 2)).reshape(-1)
    factor_all = jnp.transpose(weights, (1, 0, 2)).reshape(-1)
    block_rows = base_block.shape[0]
    offsets = targets - lax.axis_index("narrow") * block_rows
    owned = (offsets >= 0) & (offsets < block_rows)
    factors = jnp.where(owned, factor_all, 0.0)
    target_rows = jnp.where(owned, offsets, 0)
    own_block = base_block.at[target_rows].add(owner_slices.astype(jnp.float32) * factors[:, None])
    local_peak = jnp.max(own_block, axis=1)
    local_mass = jnp.sum(jnp.exp(own_block - local_peak[:, None]), axis=1)
    row_peak, row_mass = combined_all((local_peak, local_mass), "wide", merge_pair)
    log_total = row_peak + jnp.log(row_mass)
    return own_block - log_total[:, None]


def solution(mesh):
    placed = (
        P("wide", "narrow"),
        P("narrow"),
        P("narrow", "wide"),
        P("wide", "narrow", None, None),
        P(),
        P(),
        P(),
    )
    return jax.shard_map(
        body, mesh=mesh, in_specs=placed, out_specs=P("narrow", "wide"), check_vma=False
    )
```

profile of v0, /device:TPU:32, one launch (start us, length us, event | category | flops | bytes accessed | tf_op | source)
XLA Modules:
  0.0 463.4 jit_solution(9681761703783635985)
XLA Ops:
  6.5 0.0 copy-start
  6.5 0.0 all-gather.7.cloned.1.call-start
  6.5 1.0 fusion.4
  7.6 14.9 %psum.7 = f32[32]{0:T(128)S(1)} all-reduce(f32[32]{0:T(128)S(1)} %fusion.4), channel_id=1, replica_groups=mesh['wide'=64,'narrow'=8] {'narrow'}, use_global_device_ids=true, to_apply=%region_1.0 | all-reduce | flops 32 | bytes 256 | tf_op jit(solution)/shard_map/psum | solution.py:29
  22.5 1.6 fusion.6
  24.0 0.0 all-gather.7.cloned.1.call-update
  24.0 0.0 reduce-scatter.2.cloned.1.call-start
  24.1 147.9 %all-gather.7.cloned.1.call-done = bf16[2048,1024]{1,0:T(8,128)(2,1)} async-done(((bf16[32,1024]{1,0:T(8,128)(2,1)}), bf16[2048,1024]{1,0:T(8,128)(2,1)}) %all-gather.7.cloned.1.call-update) | async-done | bytes 4194320 | tf_op jit(solution)/shard_map/all_gather | solution.py:33
  172.0 0.0 copy-done
  172.0 6.5 %fusion.7 = f32[2048,500]{0,1:T(8,128)} fusion(bf16[2048,1024]{1,0:T(8,128)(2,1)} %all-gather.7.cloned.1.call-done, bf16[1024,500]{0,1:T(8,128)(2,1)S(1)} %copy-done), kind=kOutput, calls=%fused_computation.24 | convolution fusion | flops 2097152000 | bytes 9314304 | tf_op jit(solution)/shard_map/dot_general | solution.py:32
  178.5 0.0 copy-start.1
  178.5 0.0 copy-start.2
  178.5 0.0 copy-start.3
  178.5 0.0 copy-start.4
  178.5 0.0 reduce-scatter.2.cloned.1.call-update
  178.5 0.0 all-gather.9.cloned.1.call-start
  178.6 1.0 copy-done.1
  179.5 1.1 all_to_all.14
  180.7 0.3 copy.20
  181.0 32.8 %all_to_all.19 = bf16[8,64,500]{2,0,1:T(8,128)(2,1)} all-to-all(bf16[8,64,500]{2,0,1:T(8,128)(2,1)S(1)} %copy.20), channel_id=1, replica_groups=mesh['wide'=64,'narrow'=8] {'wide'}, dimensions={1} | all-to-all | bytes 1024000 | tf_op jit(solution)/shard_map/all_to_all | solution.py:38
  213.8 0.0 all-gather.9.cloned.1.call-update
  213.8 0.0 copy-done.2
  213.8 0.1 copy.19
  214.0 0.2 sub.63
  214.1 0.0 copy-done.3
  214.2 0.0 copy-done.4
  214.2 0.1 copy.21
  214.3 0.2 select_n.54
  214.5 5.4 %reduce-scatter.2.cloned.1.call-done = f32[256,500]{0,1:T(8,128)} async-done(((f32[2048,500]{0,1:T(8,128)}), f32[256,500]{0,1:T(8,128)}) %reduce-scatter.2.cloned.1.call-update) | async-done | bytes 512016 | tf_op jit(solution)/shard_map/reduce_scatter | solution.py:42
  219.9 1.2 copy.22
  221.1 39.4 %all-gather.9.cloned.1.call-done = bf16[4096,500]{1,0:T(8,128)(2,1)} async-done(((bf16[512,500]{1,0:T(8,128)(2,1)}), bf16[4096,500]{1,0:T(8,128)(2,1)}) %all-gather.9.cloned.1.call-update) | async-done | bytes 4096016 | tf_op jit(solution)/shard_map/all_gather | solution.py:43
  260.5 28.5 %scatter_custom_fusion = f32[256,500]{1,0:T(8,128)S(1)} fusion(f32[256,500]{1,0:T(8,128)S(1)} %copy.22, s32[4096]{0:T(1024)S(1)} %bitcast.35, bf16[4096,500]{1,0:T(8,128)(2,1)} %all-gather.9.cloned.1.call-done, f32[4096]{0:T(1024)S(1)} %select_n.54), kind=kCustom, calls=%fused_computation.4 | custom fusion | flops 6144000 | bytes 4624384 | tf_op jit(solution)/shard_map/scatter-add | solution.py:51
  288.9 0.2 copy.23
  289.1 0.1 reduce_max.9
  289.3 0.2 exponential_reduce_fusion
  289.5 82.5 %all-gather.2 = f32[64,1,256]{2,1,0:T(1,128)S(1)} all-gather(f32[1,1,256]{2,1,0:T(1,128)S(1)} %bitcast.36), channel_id=2, replica_groups=mesh['wide'=64,'narrow'=8] {'wide'}, dimensions={0}, use_global_device_ids=true | all-gather | bytes 66560 | tf_op jit(solution)/shard_map/all_gather | solution.py:11
  372.0 80.4 %all-gather.3 = f32[64,1,256]{2,1,0:T(1,128)S(1)} all-gather(f32[1,1,256]{2,1,0:T(1,128)S(1)} %bitcast.37), channel_id=3, replica_groups=mesh['wide'=64,'narrow'=8] {'wide'}, dimensions={0}, use_global_device_ids=true | all-gather | bytes 66560 | tf_op jit(solution)/shard_map/all_gather | solution.py:11
  452.4 3.6 while.17
  456.1 0.8 broadcast_subtract_fusion
  (135 shorter events, 2.1 us)
Async XLA Ops:
  6.5 165.5 %copy-start = (bf16[1024,500]{0,1:T(8,128)(2,1)S(1)}, bf16[1024,500]{0,1:T(8,128)(2,1)}, u32[]{:S(2)}) copy-start(bf16[1024,500]{0,1:T(8,128)(2,1)} %param.11) | copy-start | bytes 3072004
  6.5 165.5 %all-gather.7.cloned.1.call-start = ((), (), s32[]{:S(2)}) async-start(), calls=%async_computation.2 | async-start | bytes 4259840 | tf_op jit(solution)/shard_map/all_gather | solution.py:33
  24.0 195.8 %reduce-scatter.2.cloned.1.call-start = ((), (), s32[]{:S(2)}) async-start(), calls=%async_computation.3 | async-start | bytes 4644864 | tf_op jit(solution)/shard_map/reduce_scatter | solution.py:42
  178.5 1.0 copy-start.1
  178.5 35.3 %copy-start.2 = (s32[64,8,8]{0,2,1:T(8,128)S(1)}, s32[64,8,8]{0,2,1:T(8,128)}, u32[]{:S(2)}) copy-start(s32[64,8,8]{0,2,1:T(8,128)} %param.13) | copy-start | bytes 49156
  178.5 35.7 %copy-start.3 = (s32[64,8,8]{0,2,1:T(8,128)S(1)}, s32[64,8,8]{0,2,1:T(8,128)}, u32[]{:S(2)}) copy-start(s32[64,8,8]{0,2,1:T(8,128)} %param.14) | copy-start | bytes 49156
  178.5 35.7 %copy-start.4 = (s32[64,8]{0,1:T(8,128)S(1)}, s32[64,8]{0,1:T(8,128)}, u32[]{:S(2)}) copy-start(s32[64,8]{0,1:T(8,128)} %param.15) | copy-start | bytes 6148
  178.5 82.0 %all-gather.9.cloned.1.call-start = ((), (), s32[]{:S(2)}) async-start(), calls=%async_computation.4 | async-start | bytes 4718592 | tf_op jit(solution)/shard_map/all_gather | solution.py:43
Sparse Core Ops, SparseCore 0:
  24.2 147.8 all-gather.6
  178.6 41.1 reduce-scatter.1
  222.3 38.1 all-gather.8
where the time goes:
time: 464 us; the launch traced here: 463 us
  blocking collectives  211 us (45%)
  waiting for transfers between devices  193 us (42%)
  other arithmetic  33.6 us (7%)
  between operations  13.3 us (3%)
  matrix products  6.47 us (1%)
  local copies, waits for them, and re-layouts  5.1 us (1%)
    all_gather x2, blocking collectives, combined_all(): gathered = jax.tree.map(lambda a: lax.all_gather(a, axis), part)  163 us
    all_gather x1, waiting for transfers between devices, body(): lax.all_gather(normed, 'wide', axis=0, tiled=True)  148 us
    all_gather x1, waiting for transfers between devices, body(): owner_slices = lax.all_gather(arrived, 'narrow', axis=0, tiled=True)  39.4 us
    all_to_all x1, blocking collectives, body(): lax.all_to_all(row_block, 'wide', split_axis=1, concat_axis=0, tiled=True)  32.8 us
    scatter-add x1, other arithmetic, body(): base_block.at[target_rows]  28.5 us
    psum x1, blocking collectives, body(): squares = lax.psum(jnp.sum(values * values, axis=1), 'narrow')  14.9 us
  transfers between devices with their start and end apart: 3, of which 3 were waited for; matrix products, arithmetic and copies ran while one was open for 0% of the time, Pallas kernels for 0%

commit v1 on v0

--- a/solution.py
+++ b/solution.py
@@ -40,7 +40,14 @@
     active = jnp.arange(slot_total, dtype=jnp.int32)[None, None, :] < slot_count[:, :, None]
     weights = jnp.where(active, slot_code, 0).astype(jnp.float32) * 0.25
     base_block = lax.psum_scatter(partial_value, "narrow", scatter_dimension=0, tiled=True)
-    owner_slices = lax.all_gather(arrived, "narrow", axis=0, tiled=True)
+    devices = lax.axis_size("narrow")
+    right = [(i, (i + 1) % devices) for i in range(devices)]
+    parts = [arrived]
+    for far in range(1, devices):
+        parts = [lax.ppermute(parts[0], "narrow", right), *parts]
+    out = jnp.concatenate(parts, axis=0)
+    places = (lax.axis_index("narrow") + 1) * parts[-1].shape[0]
+    owner_slices = jnp.roll(out, places, axis=0)
     targets = jnp.transpose(slot_request, (1, 0, 2)).reshape(-1)
     factor_all = jnp.transpose(weights, (1, 0, 2)).reshape(-1)
     block_rows = base_block.shape[0]

time: 464 us -> 488 us (1.052)
  the two profiles are of different devices: /device:TPU:32 before, /device:TPU:2 now
where the time goes in v1:
time: 488 us; the launch traced here: 487 us
  waiting for transfers between devices  213 us (44%)
  blocking collectives  175 us (36%)
  other arithmetic  33.6 us (7%)
  local copies, waits for them, and re-layouts  25.3 us (5%)
  starting transfers between devices  18.7 us (4%)
  between operations  13.6 us (3%)
  matrix products  6.45 us (1%)
    all_gather x2, blocking collectives, combined_all(): gathered = jax.tree.map(lambda a: lax.all_gather(a, axis), part)  161 us
    all_gather x1, waiting for transfers between devices, body(): lax.all_gather(normed, 'wide', axis=0, tiled=True)  132 us
    ppermute x7, waiting for transfers between devices, body(): parts = [lax.ppermute(parts[0], 'narrow', right), *parts]  80.3 us
    scatter-add x1, other arithmetic, body(): base_block.at[target_rows]  28.5 us
    all_to_all x1, starting transfers between devices, body(): lax.all_to_all(row_block, 'wide', split_axis=1, concat_axis=0, tiled=True)  18.6 us
    unnamed x29, local copies, waits for them, and re-layouts  18.6 us
    psum x1, blocking collectives, body(): squares = lax.psum(jnp.sum(values * values, axis=1), 'narrow')  14.9 us
  transfers between devices with their start and end apart: 10, of which 8 were waited for; matrix products, arithmetic and copies ran while one was open for 5% of the time, Pallas kernels for 0%

profile of v1, /device:TPU:2, one launch (start us, length us, event | category | flops | bytes accessed | tf_op | source)
XLA Modules:
  0.0 487.5 jit_solution(7488544224328467300)
XLA Ops:
  6.5 1.0 fusion.5
  7.6 14.9 %psum.7 = f32[32]{0:T(128)S(1)} all-reduce(f32[32]{0:T(128)S(1)} %fusion.5), channel_id=1, replica_groups=mesh['wide'=64,'narrow'=8] {'narrow'}, use_global_device_ids=true, to_apply=%region_1.0 | all-reduce | flops 32 | bytes 256 | tf_op jit(solution)/shard_map/psum | solution.py:29
  22.5 1.6 fusion.7
  24.0 0.0 all-gather.6.cloned.1.call-update
  24.0 2.1 all_to_all.14
  26.1 1.1 copy.20
  27.2 18.6 %all-to-all-start = ((bf16[8,64,500]{2,0,1:T(8,128)(2,1)}), bf16[8,64,500]{2,0,1:T(8,128)(2,1)S(1)}, u32[]{:S(2)}, u32[]{:S(2)}) async-start(bf16[8,64,500]{2,0,1:T(8,128)(2,1)} %copy.20), calls=%async_computation.1 | async-start | bytes 1048576 | tf_op jit(solution)/shard_map/all_to_all | solution.py:38
  45.9 0.0 reduce-scatter.2.cloned.1.call-start
  46.0 132.4 %all-gather.6.cloned.1.call-done = bf16[2048,1024]{1,0:T(8,128)(2,1)} async-done(((bf16[32,1024]{1,0:T(8,128)(2,1)}), bf16[2048,1024]{1,0:T(8,128)(2,1)}) %all-gather.6.cloned.1.call-update) | async-done | bytes 4194320 | tf_op jit(solution)/shard_map/all_gather | solution.py:33
  178.4 6.4 %fusion.8 = f32[2048,500]{0,1:T(8,128)} fusion(bf16[2048,1024]{1,0:T(8,128)(2,1)} %all-gather.6.cloned.1.call-done, bf16[1024,500]{0,1:T(8,128)(2,1)S(1)} %copy-done), kind=kOutput, calls=%fused_computation.41 | convolution fusion | flops 2097152000 | bytes 9314304 | tf_op jit(solution)/shard_map/dot_general | solution.py:32
  184.9 0.0 collective-permute-start
  184.9 9.8 %collective-permute-done = bf16[512,500]{1,0:T(8,128)(2,1)S(1)} collective-permute-done((bf16[512,500]{1,0:T(8,128)(2,1)S(1)}, bf16[512,500]{1,0:T(8,128)(2,1)S(1)}, u32[]{:S(2)}, u32[]{:S(2)}) %collective-permute-start) | collective-permute-done | bytes 512032 | tf_op jit(solution)/shard_map/ppermute | solution.py:47
  194.7 13.9 %collective-permute-done.1 = bf16[512,500]{1,0:T(8,128)(2,1)S(1)} collective-permute-done((bf16[512,500]{1,0:T(8,128)(2,1)S(1)}, bf16[512,500]{1,0:T(8,128)(2,1)S(1)}, u32[]{:S(2)}, u32[]{:S(2)}) %collective-permute-start.1) | collective-permute-done | bytes 512032 | tf_op jit(solution)/shard_map/ppermute | solution.py:47
  208.6 15.1 %collective-permute-done.2 = bf16[512,500]{1,0:T(8,128)(2,1)S(1)} collective-permute-done((bf16[512,500]{1,0:T(8,128)(2,1)S(1)}, bf16[512,500]{1,0:T(8,128)(2,1)S(1)}, u32[]{:S(2)}, u32[]{:S(2)}) %collective-permute-start.2) | collective-permute-done | bytes 512032 | tf_op jit(solution)/shard_map/ppermute | solution.py:47
  223.8 12.0 %collective-permute-done.3 = bf16[512,500]{1,0:T(8,128)(2,1)S(1)} collective-permute-done((bf16[512,500]{1,0:T(8,128)(2,1)S(1)}, bf16[512,500]{1,0:T(8,128)(2,1)S(1)}, u32[]{:S(2)}, u32[]{:S(2)}) %collective-permute-start.3) | collective-permute-done | bytes 512032 | tf_op jit(solution)/shard_map/ppermute | solution.py:47
  235.8 0.8 copy-done.1
  236.6 9.9 %collective-permute-done.4 = bf16[512,500]{1,0:T(8,128)(2,1)} collective-permute-done((bf16[512,500]{1,0:T(8,128)(2,1)S(1)}, bf16[512,500]{1,0:T(8,128)(2,1)}, u32[]{:S(2)}, u32[]{:S(2)}) %collective-permute-start.4) | collective-permute-done | bytes 512032 | tf_op jit(solution)/shard_map/ppermute | solution.py:47
  246.6 0.1 copy.19
  246.7 0.2 sub.67
  246.9 0.1 copy.21
  247.0 0.2 select_n.69
  247.2 9.5 %collective-permute-done.5 = bf16[512,500]{1,0:T(8,128)(2,1)} collective-permute-done((bf16[512,500]{1,0:T(8,128)(2,1)}, bf16[512,500]{1,0:T(8,128)(2,1)}, u32[]{:S(2)}, u32[]{:S(2)}) %collective-permute-start.5) | collective-permute-done | bytes 512032 | tf_op jit(solution)/shard_map/ppermute | solution.py:47
  256.7 10.0 %collective-permute-done.6 = bf16[512,500]{1,0:T(8,128)(2,1)S(1)} collective-permute-done((bf16[512,500]{1,0:T(8,128)(2,1)}, bf16[512,500]{1,0:T(8,128)(2,1)S(1)}, u32[]{:S(2)}, u32[]{:S(2)}) %collective-permute-start.6) | collective-permute-done | bytes 512032 | tf_op jit(solution)/shard_map/ppermute | solution.py:47
  266.7 0.8 constant_dynamic-update-slice_fusion.15
  267.5 1.9 constant_dynamic-update-slice_fusion.14
  269.4 1.9 constant_dynamic-update-slice_fusion.13
  271.3 1.9 constant_dynamic-update-slice_fusion.12
  273.2 0.8 constant_dynamic-update-slice_fusion.11
  274.0 0.8 constant_dynamic-update-slice_fusion.10
  274.8 0.8 constant_dynamic-update-slice_fusion.9
  275.7 0.8 constant_dynamic-update-slice_fusion.8
  276.5 0.8 constant_dynamic-update-slice_fusion.7
  277.3 1.9 constant_dynamic-update-slice_fusion.6
  279.2 1.9 constant_dynamic-update-slice_fusion.5
  281.1 0.8 constant_dynamic-update-slice_fusion.4
  281.9 0.9 constant_dynamic-update-slice_fusion.3
  282.8 0.8 constant_dynamic-update-slice_fusion.2
  283.6 0.8 constant_dynamic-update-slice_fusion.1
  284.4 0.9 constant_dynamic-update-slice_fusion
  285.3 1.2 copy.22
  286.5 28.5 %scatter_custom_fusion = f32[256,500]{1,0:T(8,128)S(1)} fusion(f32[256,500]{1,0:T(8,128)S(1)} %copy.22, s32[4096]{0:T(1024)S(1)} %bitcast.37, f32[4096]{0:T(1024)S(1)} %select_n.69, bf16[8192,500]{1,0:T(8,128)(2,1)} %constant_dynamic-update-slice_fusion, s32[]{:T(128)S(6)} %select_n.66, s32[]{:T(128)} %constant.82.clone.1), kind=kCustom, calls=%fused_computation.4 | custom fusion | flops 6144000 | bytes 4723204 | tf_op jit(solution)/shard_map/scatter-add | solution.py:58
  315.0 0.1 reduce_max.9
  315.1 0.2 exponential_reduce_fusion
  315.4 80.2 %all-gather.3 = f32[64,1,256]{2,1,0:T(1,128)S(1)} all-gather(f32[1,1,256]{2,1,0:T(1,128)S(1)} %bitcast.39), channel_id=3, replica_groups=mesh['wide'=64,'narrow'=8] {'wide'}, dimensions={0}, use_global_device_ids=true | all-gather | bytes 66560 | tf_op jit(solution)/shard_map/all_gather | solution.py:11
  395.6 80.3 %all-gather.2 = f32[64,1,256]{2,1,0:T(1,128)S(1)} all-gather(f32[1,1,256]{2,1,0:T(1,128)S(1)} %bitcast.38), channel_id=2, replica_groups=mesh['wide'=64,'narrow'=8] {'wide'}, dimensions={0}, use_global_device_ids=true | all-gather | bytes 66560 | tf_op jit(solution)/shard_map/all_gather | solution.py:11
  475.9 0.2 copy.23
  476.1 3.6 while.17
  479.8 0.8 broadcast_subtract_fusion
  (156 shorter events, 2.1 us)
Async XLA Ops:
  6.5 171.9 %copy-start = (bf16[1024,500]{0,1:T(8,128)(2,1)S(1)}, bf16[1024,500]{0,1:T(8,128)(2,1)}, u32[]{:S(2)}) copy-start(bf16[1024,500]{0,1:T(8,128)(2,1)} %param.11) | copy-start | bytes 3072004
  6.5 171.9 %all-gather.6.cloned.1.call-start = ((), (), s32[]{:S(2)}) async-start(), calls=%async_computation.2 | async-start | bytes 4259840 | tf_op jit(solution)/shard_map/all_gather | solution.py:33
  27.2 157.6 %all-to-all-start = ((bf16[8,64,500]{2,0,1:T(8,128)(2,1)}), bf16[8,64,500]{2,0,1:T(8,128)(2,1)S(1)}, u32[]{:S(2)}, u32[]{:S(2)}) async-start(bf16[8,64,500]{2,0,1:T(8,128)(2,1)} %copy.20), calls=%async_computation.1 | async-start | bytes 1048576 | tf_op jit(solution)/shard_map/all_to_all | solution.py:38
  45.9 200.7 %copy-start.3 = (s32[64,8,8]{0,2,1:T(8,128)S(1)}, s32[64,8,8]{0,2,1:T(8,128)}, u32[]{:S(2)}) copy-start(s32[64,8,8]{0,2,1:T(8,128)} %param.13) | copy-start | bytes 49156
  45.9 201.0 %copy-start.4 = (s32[64,8,8]{0,2,1:T(8,128)S(1)}, s32[64,8,8]{0,2,1:T(8,128)}, u32[]{:S(2)}) copy-start(s32[64,8,8]{0,2,1:T(8,128)} %param.14) | copy-start | bytes 49156
  45.9 201.0 %copy-start.5 = (s32[64,8]{0,1:T(8,128)S(1)}, s32[64,8]{0,1:T(8,128)}, u32[]{:S(2)}) copy-start(s32[64,8]{0,1:T(8,128)} %param.15) | copy-start | bytes 6148
  45.9 239.4 %reduce-scatter.2.cloned.1.call-start = ((), (), s32[]{:S(2)}) async-start(), calls=%async_computation.3 | async-start | bytes 4644864 | tf_op jit(solution)/shard_map/reduce_scatter | solution.py:42
  184.9 9.8 %collective-permute-start = (bf16[512,500]{1,0:T(8,128)(2,1)S(1)}, bf16[512,500]{1,0:T(8,128)(2,1)S(1)}, u32[]{:S(2)}, u32[]{:S(2)}) collective-permute-start(bf16[512,500]{1,0:T(8,128)(2,1)S(1)} %bitcast.30), channel_id=1, source_target_pairs={{0,1},{1,2},{2,3},{3,4},{4,5},{5,6},{6,7},{7,0},{8,9},{9,10},{10,1... | collective-permute-start | bytes 1536008 | tf_op jit(solution)/shard_map/ppermute | solution.py:47
  194.7 13.9 %collective-permute-start.1 = (bf16[512,500]{1,0:T(8,128)(2,1)S(1)}, bf16[512,500]{1,0:T(8,128)(2,1)S(1)}, u32[]{:S(2)}, u32[]{:S(2)}) collective-permute-start(bf16[512,500]{1,0:T(8,128)(2,1)S(1)} %collective-permute-done), channel_id=1, source_target_pairs={{0,1},{1,2},{2,3},{3,4},{4,5},{5,6},{6,7},{7,0},{8,9},{9,10},{10,1... | collective-permute-start | bytes 1536008 | tf_op jit(solution)/shard_map/ppermute | solution.py:47
  208.6 15.1 %collective-permute-start.2 = (bf16[512,500]{1,0:T(8,128)(2,1)S(1)}, bf16[512,500]{1,0:T(8,128)(2,1)S(1)}, u32[]{:S(2)}, u32[]{:S(2)}) collective-permute-start(bf16[512,500]{1,0:T(8,128)(2,1)S(1)} %collective-permute-done.1), channel_id=1, source_target_pairs={{0,1},{1,2},{2,3},{3,4},{4,5},{5,6},{6,7},{7,0},{8,9},{9,10},{10,1... | collective-permute-start | bytes 1536008 | tf_op jit(solution)/shard_map/ppermute | solution.py:47
  223.8 12.0 %collective-permute-start.3 = (bf16[512,500]{1,0:T(8,128)(2,1)S(1)}, bf16[512,500]{1,0:T(8,128)(2,1)S(1)}, u32[]{:S(2)}, u32[]{:S(2)}) collective-permute-start(bf16[512,500]{1,0:T(8,128)(2,1)S(1)} %collective-permute-done.2), channel_id=1, source_target_pairs={{0,1},{1,2},{2,3},{3,4},{4,5},{5,6},{6,7},{7,0},{8,9},{9,10},{10,1... | collective-permute-start | bytes 1536008 | tf_op jit(solution)/shard_map/ppermute | solution.py:47
  235.8 0.8 copy-start.1
  236.6 9.9 %collective-permute-start.4 = (bf16[512,500]{1,0:T(8,128)(2,1)S(1)}, bf16[512,500]{1,0:T(8,128)(2,1)}, u32[]{:S(2)}, u32[]{:S(2)}) collective-permute-start(bf16[512,500]{1,0:T(8,128)(2,1)S(1)} %collective-permute-done.3), channel_id=1, source_target_pairs={{0,1},{1,2},{2,3},{3,4},{4,5},{5,6},{6,7},{7,0},{8,9},{9,10},{10,1... | collective-permute-start | bytes 1536008 | tf_op jit(solution)/shard_map/ppermute | solution.py:47
  246.5 10.1 %collective-permute-start.5 = (bf16[512,500]{1,0:T(8,128)(2,1)}, bf16[512,500]{1,0:T(8,128)(2,1)}, u32[]{:S(2)}, u32[]{:S(2)}) collective-permute-start(bf16[512,500]{1,0:T(8,128)(2,1)} %collective-permute-done.4), channel_id=1, source_target_pairs={{0,1},{1,2},{2,3},{3,4},{4,5},{5,6},{6,7},{7,0},{8,9},{9,10},{10,1... | collective-permute-start | bytes 1536008 | tf_op jit(solution)/shard_map/ppermute | solution.py:47
  247.2 33.9 %copy-start.2 = (bf16[512,500]{1,0:T(8,128)(2,1)S(1)}, bf16[512,500]{1,0:T(8,128)(2,1)}, u32[]{:S(2)}) copy-start(bf16[512,500]{1,0:T(8,128)(2,1)} %copy-done.1) | copy-start | bytes 1536004
  256.7 10.0 %collective-permute-start.6 = (bf16[512,500]{1,0:T(8,128)(2,1)}, bf16[512,500]{1,0:T(8,128)(2,1)S(1)}, u32[]{:S(2)}, u32[]{:S(2)}) collective-permute-start(bf16[512,500]{1,0:T(8,128)(2,1)} %collective-permute-done.5), channel_id=1, source_target_pairs={{0,1},{1,2},{2,3},{3,4},{4,5},{5,6},{6,7},{7,0},{8,9},{9,10},{10,1... | collective-permute-start | bytes 1536008 | tf_op jit(solution)/shard_map/ppermute | solution.py:47
Sparse Core Ops, SparseCore 0:
  24.2 154.1 all-gather.5
  185.0 49.0 reduce-scatter.1
